TPU v7x, 256 devices: a whole 4x4x8 slice. The times are simulated.
256 devices in a mesh: comp: 2 (over core), gx: 32 (over x, z), gy: 4 (over y).
Axes of the slice: x: 4, y: 4, z: 8, core: 2. Of those that a mesh axis runs over, the one named last changes fastest.
Arguments:
- theta: float32 [2, 48, 1024, 512], P('comp', None, 'gx', 'gy'), may hold values from -0.5 to 1.5
- surface: float32 [2, 1024, 512], P('comp', 'gx', 'gy'), may hold values from -6 to 6
- kappa: float32 [2, 1024, 512], P('comp', 'gx', 'gy'), may hold values from 0.005 to 0.05
- depth: float32 [1024, 512], P('gx', 'gy'), may hold values from 0.2 to 1
- wet: int32 [1024, 512], P('gx', 'gy'), may hold values 0 or 1
- remap_ids: int32 [2, 256, 128, 8], P('comp', 'gx', 'gy'), may hold values from 0 to 32767, as said below
- remap_counts: int32 [2, 256, 128], P('comp', 'gx', 'gy'), may hold values from 1 to 8
- remap_weights: bfloat16 [2, 256, 128, 16, 128], P('comp', 'gx', 'gy'), may hold values from -0.5 to 0.5
Outputs:
- theta_out: float32 [2, 48, 1024, 512], P('comp', None, 'gx', 'gy')
- surface_out: float32 [2, 1024, 512], P('comp', 'gx', 'gy')
Inputs may be any that keep to these rules, and one draw needn't show every extreme that they name: `remap_ids`: tiles of a component are numbered id = (device * tiles of a device) + tile, device = gx index * (devices along gy) + gy index, tile row-major over the device's 32/4 x 128/4 tiles. Every id lies on a device whose gx index is within 1 of the destination tile's device, cyclically; both distances +1 and -1 occur on every destination device. Slots at or beyond a tile's count are ignored.
All inputs are finite; a program needn't handle non-finite values. No bound on the sum of `wet` on one device may be relied on, other than what follows from the above.
Results may differ from a plain program's by a relative error of at most 0.0003.
Values sent between devices are 32-bit elements; how exact they have to be, the bound alone decides.
A program may use at most 128 MiB of HBM per device.

v0:
```python
import functools

import jax
import jax.numpy as jnp
import ml_dtypes
import numpy as np
from jax import lax
from jax.experimental import pallas as pl
from jax.experimental.pallas import tpu as pltpu
from jax.sharding import PartitionSpec as P

MESH = pl.DeviceIdType.MESH
F32 = jnp.float32
BF16 = jnp.bfloat16

NSTEP = 6
ITERS = 4
SLOTS = 8
LEV = 48
CX = 32
CY = 128
ROWS = 56
SURF = 48

node_derivative = np.array(
    [
        [-3.0, 4.045084971874737, -1.545084971874737, 0.5],
        [-0.809016994374947, 0.0, 1.118033988749895, -0.309016994374947],
        [0.309016994374947, -1.118033988749895, 0.0, 0.809016994374947],
        [-0.5, 1.545084971874737, -4.045084971874737, 3.0],
    ]
)
second_derivative = node_derivative @ node_derivative
vertical_mix = 0.2
heat_rate = 0.5
air_rate = 0.3
press_rate = 0.1
damping = 0.05
fresh_rate = 0.5
bound_low = 0.02
bound_high = 2.0


def heat_response():
    level = np.zeros(LEV)
    for _ in range(NSTEP):
        change = level[1:] - level[:-1]
        level = level + vertical_mix * (np.append(change, 0.0) - np.append(0.0, change))
        level[0] += heat_rate
    return [float(v) for v in level]


def halves(table):
    high = table.astype(ml_dtypes.bfloat16)
    low = (table - high.astype(np.float64)).astype(ml_dtypes.bfloat16)
    return high, low


def tables():
    lane = np.arange(256)
    f_in, dx_in, dy_in = (lane // 64) % 2, (lane // 16) % 4, lane % 4
    f_out, dx_out, dy_out = lane // 128, (lane // 4) % 4, lane % 4
    fold = (
        (f_in[:, None] == f_out[None])
        & (dx_in[:, None] == dx_out[None])
        & (dy_in[:, None] == dy_out[None])
    )
    block = np.kron(np.eye(32), second_derivative.T)
    high, low = halves(block)
    zero = np.zeros((128, 128))
    lap = np.block(
        [[high.astype(np.float64), low.astype(np.float64)], [high.astype(np.float64), zero]]
    )
    lane = np.arange(128)
    target = ((lane // 4) % 4) * 32 + (lane // 16) * 4 + lane % 4
    perm = np.zeros((128, 256))
    perm[lane, target] = 1.0
    return np.concatenate([fold.astype(np.float64), lap, perm]).astype(ml_dtypes.bfloat16)


def split(value):
    high = value.astype(BF16)
    low = (value - high.astype(F32)).astype(BF16)
    return high, low


def dot(a, b):
    return jnp.dot(a, b, preferred_element_type=F32)


def radices(count):
    if count == 32:
        return [4, 2, 4]
    found = []
    while count > 1:
        size = 4 if count % 4 == 0 else count
        found.append(size)
        count //= size
    return found


def kernel(
    n_gx,
    n_gy,
    theta,
    surface,
    kappa,
    depth,
    wet,
    ids,
    counts,
    weights,
    consts,
    theta_out,
    surface_out,
    fp,
    ys,
    yr,
    zb,
    ex,
    tsend,
    trecv,
    table,
    wbuf,
    cbuf,
    idbuf,
    cntbuf,
    wetbuf,
    coef,
    pb,
    dbuf,
    imp,
    pcr,
    grid,
    red,
    redr,
    lsem,
    hs,
    hr,
    es,
    er,
    rs,
    rr,
):
    comp = lax.axis_index("comp")
    gx = lax.axis_index("gx")
    gy = lax.axis_index("gy")
    sources = 3 * n_gy
    units = (CX // 4) * (CY // 4)
    is_ocean = comp == 0
    is_air = comp == 1
    has_south = gy > 0
    has_north = gy < n_gy - 1

    def place(dc, dx, dy):
        return (lax.rem(comp + dc, 2), lax.rem(gx + dx + n_gx, n_gx), lax.rem(gy + dy + n_gy, n_gy))

    halo_peers = [
        place(0, 1, 0),
        place(0, -1, 0),
        place(0, 0, 1),
        place(0, 0, -1),
        place(0, 1, 1),
        place(0, -1, 1),
        place(0, 1, -1),
        place(0, -1, -1),
    ]
    export_peers = [(d, j, place(1, d, j)) for d in (-1, 0, 1) for j in range(n_gy)]
    sum_phases = []
    sum_phases.append([place(dc, 0, j) for dc in range(2) for j in range(n_gy) if dc or j])
    stride = 1
    for size in radices(n_gx):
        digit = lax.rem(gx // stride, size)
        group = []
        for j in range(1, size):
            group.append((comp, gx + (lax.rem(digit + j, size) - digit) * stride, gy))
        sum_phases.append(group)
        stride *= size

    loads = {}

    def load(name, index, src, dst):
        copy = pltpu.make_async_copy(src, dst, lsem.at[index])
        copy.start()
        loads.setdefault(name, []).append(copy)

    def loaded(name):
        for copy in loads.pop(name):
            copy.wait()

    load("export", 0, theta.at[0, 0], grid.at[0])
    load("export", 1, surface.at[0], grid.at[1])
    load("export", 2, wet, wetbuf)
    load("export", 3, kappa.at[0], grid.at[2])
    load("export", 4, depth, grid.at[3])
    for x in range(CX):
        load("theta", 8 + x, theta.at[0, :, x, :], fp.at[0, x + 1, pl.ds(0, LEV), :])
    load("remap", 5, ids.at[0], idbuf)
    load("remap", 6, counts.at[0], cntbuf)
    load("tables", 7, consts, cbuf)
    load("weights", 40, weights.at[0], wbuf)

    barrier = pltpu.get_barrier_semaphore()
    greeted = halo_peers + [p for _, _, p in export_peers] + [p for g in sum_phases for p in g]
    for peer in greeted:
        pl.semaphore_signal(barrier, inc=1, device_id=peer, device_id_type=MESH)

    lane128 = lax.broadcasted_iota(jnp.int32, (8, 128), 1)
    lane1 = lax.broadcasted_iota(jnp.int32, (1, 128), 1)

    loaded("export")
    wet_float = wetbuf[...].astype(F32)
    grid[4] = wet_float
    top = grid[0]

    ex[0] = jnp.where(is_ocean, top * wet_float, top)
    ex[1] = jnp.where(is_ocean, wet_float, grid[1])
    parts = [ex[f, pl.ds(dx, 8, stride=4), :] for f in range(2) for dx in range(4)]
    for h in range(8):
        acc = jnp.zeros((8, 128), F32)
        for j in range(8):
            shift = ((j - h) * 16) % 128
            moved = pltpu.roll(parts[j], shift, 1) if shift else parts[j]
            acc = jnp.where(lane128 // 16 == j, moved, acc)
        tsend[pl.ds(8 * h, 8), :] = acc

    for x in range(CX):
        fp[0, x + 1, SURF : SURF + 1, :] = grid[1, x : x + 1, :]
        fp[0, x + 1, SURF + 1 : SURF + 2, :] = grid[2, x : x + 1, :]
        fp[0, x + 1, SURF + 2 : SURF + 3, :] = grid[3, x : x + 1, :]
        fp[0, x + 1, SURF + 3 : SURF + 4, :] = grid[4, x : x + 1, :]
        fp[0, x + 1, SURF + 4 : SURF + 8, :] = jnp.zeros((4, 128), F32)

    def pack(s):
        def body(x, accs):
            accs = list(accs)
            for b in range(7):
                base = 2 * x + 64 * (b % 2)
                moved = pltpu.roll(fp[s, x + 1, 8 * b : 8 * b + 8, :], base + 1, 1)
                accs[b // 2] = jnp.where(
                    (lane128 == base) | (lane128 == base + 1), moved, accs[b // 2]
                )
            return tuple(accs)

        zero = jnp.zeros((8, 128), F32)
        accs = lax.fori_loop(0, CX, body, (zero,) * 4)
        for j in range(4):
            ys[s, j] = accs[j]

    def copy_to(s, d):
        if d == 0:
            src, dst, peer = fp.at[s, CX], fp.at[s, 0], halo_peers[0]
        elif d == 1:
            src, dst, peer = fp.at[s, 1], fp.at[s, CX + 1], halo_peers[1]
        else:
            src, dst, peer = ys.at[s], yr.at[s, d - 2], halo_peers[d]
        return pltpu.make_async_remote_copy(
            src_ref=src,
            dst_ref=dst,
            send_sem=hs.at[s, d],
            recv_sem=hr.at[s, d],
            device_id=peer,
            device_id_type=MESH,
        )

    def send_halo(s):
        for d in range(4):
            copy_to(s, d).start()

        @pl.when(is_air)
        def _():
            for d in range(4, 8):
                copy_to(s, d).start()

    def wait_halo(s):
        for d in range(4):
            copy_to(s, d).wait_recv()

        @pl.when(is_air)
        def _():
            for d in range(4, 8):
                copy_to(s, d).wait_recv()

    def drain_halo(s):
        for d in range(4):
            copy_to(s, d).wait_send()

        @pl.when(is_air)
        def _():
            for d in range(4, 8):
                copy_to(s, d).wait_send()

    def merged(s, south, north):
        found = []
        for j in range(4):
            low = yr[s, south, j]
            high = pltpu.roll(yr[s, north, j], 126, 1)
            found.append(jnp.where(lane128 % 2 == 0, low, high))
        return found

    def unpack(s, corners):
        own = merged(s, 0, 1)

        def fill(x, vectors, slab):
            for b in range(7):
                shift = lax.rem(256 - 2 * x - 64 * (b % 2), 128)
                zb[slab, 8 * b : 8 * b + 8, :] = pltpu.roll(vectors[b // 2], shift, 1)

        def body(x, carry):
            fill(x, own, x + 1)
            return carry

        lax.fori_loop(0, CX, body, 0)
        if corners:
            fill(CX - 1, merged(s, 2, 4), 0)
            fill(0, merged(s, 3, 5), CX + 1)

    def export_copy(d, j, peer):
        slot = (1 - d) * n_gy + gy
        return pltpu.make_async_remote_copy(
            src_ref=tsend,
            dst_ref=trecv.at[slot],
            send_sem=es.at[(d + 1) * n_gy + j],
            recv_sem=er.at[slot],
            device_id=peer,
            device_id_type=MESH,
        )

    loaded("theta")
    pack(0)
    pl.semaphore_wait(barrier, len(greeted))
    for d, j, peer in export_peers:
        export_copy(d, j, peer).start()
    send_halo(0)

    loaded("remap")
    loaded("tables")
    cnt = cntbuf[...].astype(F32)
    lane32 = lax.broadcasted_iota(jnp.int32, (32, 32), 1)
    row32 = lax.broadcasted_iota(jnp.int32, (32, 32), 0)
    ones = jnp.ones((32, 128), BF16)
    counted = []
    for tx in range(8):
        spread = jnp.where(lane32 == row32, jnp.broadcast_to(cnt[tx : tx + 1, :], (32, 32)), 0.0)
        counted.append(dot(spread.astype(BF16), ones)[:, :SLOTS])
    counted = jnp.concatenate(counted, axis=0)
    id_all = idbuf[...].reshape(units, SLOTS)
    slot_lane = lax.broadcasted_iota(jnp.int32, (units, SLOTS), 1)
    dev = id_all // units
    unit = id_all - dev * units
    dev_gx = dev // n_gy
    dev_gy = dev - dev_gx * n_gy
    tile_x = unit // 32
    tile_y = unit - tile_x * 32
    offset = dev_gx - gx + 1
    offset = jnp.where(offset < 0, offset + n_gx, jnp.where(offset >= n_gx, offset - n_gx, offset))
    key = (offset * n_gy + dev_gy) * 64 + (tile_y // 4) * 8 + tile_x
    key = jnp.where(slot_lane.astype(F32) < counted, key, -1)
    tile_low = tile_y - (tile_y // 4) * 4

    wait_halo(0)
    unpack(0, True)

    def rims(s, row):
        pass

    def lanes_of(shape):
        return lax.broadcasted_iota(jnp.int32, shape, 1)

    lane_full = lanes_of((CX, CY))

    def gather_row(s, row, slot):
        for x in range(CX):
            grid[slot, x : x + 1, :] = fp[s, x + 1, row : row + 1, :]

    def rim_row(row, slot):
        for x in range(CX):
            grid[slot, x : x + 1, :] = zb[x + 1, row : row + 1, :]

    def shifted(center, west_row, east_row, rim):
        row_place = lax.broadcasted_iota(jnp.int32, (CX, CY), 0)
        east = jnp.where(row_place == CX - 1, east_row, pltpu.roll(center, CX - 1, 0))
        west = jnp.where(row_place == 0, west_row, pltpu.roll(center, 1, 0))
        north = jnp.where(lane_full == CY - 1, rim, pltpu.roll(center, CY - 1, 1))
        south = jnp.where(lane_full == 0, rim, pltpu.roll(center, 1, 1))
        return east, west, north, south

    def side_rows(s, row):
        return fp[s, 0, row : row + 1, :], fp[s, CX + 1, row : row + 1, :]

    @pl.when(is_ocean)
    def _():
        wet_c = grid[4]
        rim_row(SURF + 3, 5)
        we, ww, wn, ws = shifted(wet_c, *side_rows(0, SURF + 3), grid[5])
        wn = jnp.where((lane_full == CY - 1) & jnp.logical_not(has_north), 0.0, wn)
        ws = jnp.where((lane_full == 0) & jnp.logical_not(has_south), 0.0, ws)
        for row, slot, at in ((SURF + 1, 2, 0), (SURF + 2, 3, 6)):
            center = grid[slot]
            rim_row(row, 5)
            ke, kw, kn, ks = shifted(center, *side_rows(0, row), grid[5])
            base = center * wet_c
            coef[at] = 0.5 * (base + ke * we) * wet_c * we
            coef[at + 1] = 0.5 * (kw * ww + base) * ww * wet_c
            coef[at + 2] = 0.5 * (base + kn * wn) * wet_c * wn
            coef[at + 3] = 0.5 * (ks * ws + base) * ws * wet_c
        coef[4] = (
            1.0 - (coef[0] + coef[1] + coef[2] + coef[3]) - (2.0 * vertical_mix) * wet_c
        )
        coef[5] = vertical_mix * wet_c
        diagonal = damping + coef[6] + coef[7] + coef[8] + coef[9]
        coef[10] = diagonal
        main = wet_c * diagonal + (1.0 - wet_c)
        lower = jnp.where(lane_full == 0, 0.0, -coef[9])
        upper = jnp.where(lane_full == CY - 1, 0.0, -coef[8])
        step = 1
        index = 0
        while step < CY:
            back = CY - step
            below_main = pltpu.roll(main, step, 1)
            above_main = pltpu.roll(main, back, 1)
            factor_below = -lower / below_main
            factor_above = -upper / above_main
            pcr[index] = factor_below
            pcr[index + 1] = factor_above
            main = (
                main
                + factor_below * pltpu.roll(upper, step, 1)
                + factor_above * pltpu.roll(lower, back, 1)
            )
            lower = factor_below * pltpu.roll(lower, step, 1)
            upper = factor_above * pltpu.roll(upper, back, 1)
            step *= 2
            index += 2
        pcr[14] = 1.0 / main

    def solve(values):
        step = 1
        index = 0
        while step < CY:
            values = (
                values
                + pcr[index] * pltpu.roll(values, step, 1)
                + pcr[index + 1] * pltpu.roll(values, CY - step, 1)
            )
            step *= 2
            index += 2
        return values * pcr[14]

    lane56 = lanes_of((ROWS, CY))
    row56 = lax.broadcasted_iota(jnp.int32, (ROWS, CY), 0)
    row48 = lax.broadcasted_iota(jnp.int32, (LEV, CY), 0)
    lane48 = lanes_of((LEV, CY))

    def ocean_step(s):
        def body(x, carry):
            c = fp[s - 1, x + 1, 0:LEV, :]
            w = fp[s - 1, x, 0:LEV, :]
            e = fp[s - 1, x + 2, 0:LEV, :]
            z = zb[x + 1, 0:LEV, :]

            def row(i):
                return coef[i, pl.ds(x, 1), :]

            n = jnp.where(lane48 == CY - 1, z, pltpu.roll(c, CY - 1, 1))
            o = jnp.where(lane48 == 0, z, pltpu.roll(c, 1, 1))
            up = jnp.where(row48 == LEV - 1, c, pltpu.roll(c, LEV - 1, 0))
            down = jnp.where(row48 == 0, c, pltpu.roll(c, 1, 0))
            new = (
                row(4) * c
                + row(0) * e
                + row(1) * w
                + row(2) * n
                + row(3) * o
                + row(5) * (up + down)
            )
            fp[s, x + 1, 0:LEV, :] = new
            if s > 1:
                fp[s, x + 1, 0:1, :] = new[0:1, :] + grid[7, pl.ds(x, 1), :]
            return carry

        lax.fori_loop(0, CX, body, 0)

    def air_step(s):
        h = jnp.where(
            ((lane1 % 4 == 0) & ((lane1 > 0) | has_south))
            | ((lane1 % 4 == 3) & ((lane1 < CY - 1) | has_north)),
            0.5,
            0.0,
        )
        mix_up = jnp.where(row56 < LEV - 1, vertical_mix, 0.0)
        mix_down = jnp.where((row56 > 0) & (row56 < LEV), vertical_mix, 0.0)

        def body(i, carry):
            x0 = 4 * i
            v = [fp[s - 1, x0 + j] for j in range(6)]
            z = [zb[x0 + j] for j in range(6)]

            def across(t):
                return [0.5 * (t[1] + t[0]), t[2], t[3], 0.5 * (t[4] + t[5])]

            blocks = []
            for a, za in zip(across(v), across(z)):
                partner = jnp.where(lane56 % 4 == 0, pltpu.roll(a, 1, 1), pltpu.roll(a, CY - 1, 1))
                partner = jnp.where((lane56 == 0) | (lane56 == CY - 1), za, partner)
                blocks.append(a + h * (partner - a))
            high, low = split(jnp.concatenate(blocks, axis=0))
            along = dot(jnp.concatenate([high, low], axis=1), cbuf[256:512, :])
            along = along[:, :CY] + along[:, CY:]
            for j in range(4):
                b = blocks[j]
                lap = along[ROWS * j : ROWS * (j + 1)]
                for m in range(4):
                    lap = lap + float(second_derivative[j, m]) * blocks[m]
                up = pltpu.roll(b, ROWS - 1, 0)
                down = pltpu.roll(b, 1, 0)
                new = (
                    b
                    + grid[2, pl.ds(x0 + j, 1), :] * lap
                    + mix_up * (up - b)
                    + mix_down * (down - b)
                )
                x = x0 + j
                fp[s, x + 1] = new
                if s == 1:
                    grid[8, pl.ds(x, 1), :] = b[0:1, :]
                    grid[9, pl.ds(x, 1), :] = b[SURF : SURF + 1, :]
                else:
                    fp[s, x + 1, 0:1, :] = (
                        new[0:1, :]
                        + grid[6, pl.ds(x, 1), :]
                        - grid[7, pl.ds(x, 1), :] * b[0:1, :]
                    )
                    if s <= ITERS:
                        fp[s, x + 1, SURF : SURF + 1, :] = (
                            new[SURF : SURF + 1, :]
                            + grid[10, pl.ds(x, 1), :]
                            - press_rate * b[SURF : SURF + 1, :]
                        )
            return carry

        lax.fori_loop(0, CX // 4, body, 0)

    def forward(s):
        @pl.when(is_ocean)
        def _():
            ocean_step(s)

        @pl.when(is_air)
        def _():
            air_step(s)

    forward(1)

    for d in range(3):
        for j in range(n_gy):
            slot = d * n_gy + j
            pltpu.make_async_remote_copy(
                src_ref=tsend,
                dst_ref=trecv.at[slot],
                send_sem=es.at[slot],
                recv_sem=er.at[slot],
                device_id=halo_peers[0],
                device_id_type=MESH,
            ).wait_recv()
    high, low = split(trecv[...].reshape(sources * 64, 128))
    table[:, 0:128] = high
    table[:, 128:256] = low
    key_lane = lax.broadcasted_iota(jnp.int32, (units, sources * 64), 1)
    lane256 = lax.broadcasted_iota(jnp.int32, (units, 256), 1)
    low_lane = (lane256 // 4) % 4
    slot_of = (lane256 // 16) % 8
    picked = jnp.zeros((units, 256), F32)
    for m in range(SLOTS):
        hot = jnp.where(key[:, m : m + 1] == key_lane, 1.0, 0.0).astype(BF16)
        found = dot(hot, table[...])
        found = jnp.where(low_lane == tile_low[:, m : m + 1], found, 0.0).astype(BF16)
        picked = jnp.where(slot_of == m, dot(found, cbuf[0:256, :]), picked)
    high, low = split(picked)
    pb[0] = high[:, 0:128]
    pb[1] = high[:, 128:256]
    pb[2] = low[:, 0:128]
    pb[3] = low[:, 128:256]
    loaded("weights")
    own_tile = lax.broadcasted_iota(jnp.int32, (16, 256), 0) == (
        lax.broadcasted_iota(jnp.int32, (16, 256), 1) // 16
    )
    for g in range(16):
        left = pb[:, 16 * g : 16 * g + 16, :].reshape(64, 128)
        right = wbuf[g // 2, 16 * (g % 2) : 16 * (g % 2) + 16].reshape(256, 128)
        out = lax.dot_general(
            left, right, (((1,), (1,)), ((), ())), preferred_element_type=F32
        )
        for f in range(2):
            value = out[16 * f : 16 * f + 16] + out[32 + 16 * f : 48 + 16 * f]
            value = jnp.sum(jnp.where(own_tile, value, 0.0), axis=0, keepdims=True)
            for u in range(2):
                dbuf[f, 2 * (g % 2) + u, g // 2 : g // 2 + 1, :] = value[:, 128 * u : 128 * u + 128]
    high, low = split(dbuf[...].reshape(64, 128))
    turned = dot(jnp.concatenate([high, low], axis=0), cbuf[512:640, 0:128])
    turned = turned[:64] + turned[64:]
    for f in range(2):
        quarters = [turned[32 * f + 8 * q : 32 * f + 8 * q + 8] for q in range(4)]
        for dx in range(4):
            acc = jnp.zeros((8, 128), F32)
            for q in range(4):
                shift = ((q - dx) * 32) % 128
                moved = pltpu.roll(quarters[q], shift, 1) if shift else quarters[q]
                acc = jnp.where(lane128 // 32 == q, moved, acc)
            imp[f, pl.ds(dx, 8, stride=4), :] = acc

    wet_c = grid[4]
    heat = jnp.where(is_ocean, -(wet_c * imp[0]), grid[0])
    cells = jnp.where(is_ocean, wet_c, 0.0)
    row8 = lax.broadcasted_iota(jnp.int32, (8, 128), 0)

    def rows8(v):
        return jnp.sum(v, axis=0, keepdims=True)

    red[0] = jnp.where(row8 == 0, rows8(heat), jnp.where(row8 == 1, rows8(cells), 0.0))

    def sum_copy(phase, j):
        return pltpu.make_async_remote_copy(
            src_ref=red.at[phase],
            dst_ref=redr.at[phase, j],
            send_sem=rs.at[phase, j],
            recv_sem=rr.at[phase, j],
            device_id=sum_phases[phase][j],
            device_id_type=MESH,
        )

    def sum_send(phase):
        for j in range(len(sum_phases[phase])):
            sum_copy(phase, j).start()

    def sum_finish(phase):
        total = red[phase]
        for j in range(len(sum_phases[phase])):
            sum_copy(phase, j).wait_recv()
            total = total + redr[phase, j]
        red[phase + 1] = total

    sum_send(0)

    centre = (bound_high + bound_low) / 2.0
    half_range = (bound_high - bound_low) / 2.0
    spread_ratio = centre / half_range

    def apply_a(s, center):
        rim_row(SURF, 5)
        east, west, north, south = shifted(center, *side_rows(s, SURF), grid[5])
        near = coef[6] * east + coef[7] * west + coef[8] * north + coef[9] * south
        return wet_c * (coef[10] * center - near) + (1.0 - wet_c) * center

    def put_surface(s, value):
        grid[13] = value
        for x in range(CX):
            fp[s, x + 1, SURF : SURF + 1, :] = grid[13, x : x + 1, :]

    @pl.when(is_ocean)
    def _():
        force = heat_rate * wet_c * imp[0]
        grid[7] = force
        for x in range(CX):
            fp[1, x + 1, 0:1, :] = fp[1, x + 1, 0:1, :] + grid[7, x : x + 1, :]
        eta = grid[1]
        residual = wet_c * (damping * eta + fresh_rate * imp[1]) - apply_a(0, eta)
        direction = solve(residual) / centre
        grid[11] = eta + direction
        grid[12] = residual
        put_surface(1, direction)

    @pl.when(is_air)
    def _():
        grid[6] = air_rate * imp[0]
        grid[7] = air_rate * imp[1]
        grid[10] = press_rate * imp[0]
        grid[5] = grid[6] - grid[7] * grid[8]
        grid[11] = grid[10] - press_rate * grid[9]
        for x in range(CX):
            fp[1, x + 1, 0:1, :] = fp[1, x + 1, 0:1, :] + grid[5, x : x + 1, :]
            fp[1, x + 1, SURF : SURF + 1, :] = (
                fp[1, x + 1, SURF : SURF + 1, :] + grid[11, x : x + 1, :]
            )

    recurrence = 1.0 / spread_ratio
    phases = len(sum_phases)
    for s in range(2, NSTEP + 1):
        pack(s - 1)
        send_halo(s - 1)
        if s - 2 >= 1 and s - 2 < phases:
            sum_send(s - 2)
        wait_halo(s - 1)
        if s - 2 < phases:
            sum_finish(s - 2)
        unpack(s - 1, True)
        forward(s)
        if s <= ITERS:
            recurrence_next = 1.0 / (2.0 * spread_ratio - recurrence)

            @pl.when(is_ocean)
            def _(s=s, recurrence=recurrence, recurrence_next=recurrence_next):
                old = grid[13]
                residual = grid[12] - apply_a(s - 1, old)
                direction = (recurrence_next * recurrence) * old + (
                    2.0 * recurrence_next / half_range
                ) * solve(residual)
                grid[11] = grid[11] + direction
                grid[12] = residual
                put_surface(s, direction)

            recurrence = recurrence_next
        if s == ITERS:

            @pl.when(is_air)
            def _(s=s):
                gather_row(s, SURF, 11)

            loads["surface"] = [pltpu.make_async_copy(grid.at[11], surface_out.at[0], lsem.at[41])]
            loads["surface"][0].start()

    total = red[phases]
    correction = jnp.sum(total[0:1, :], axis=1, keepdims=True) / jnp.sum(
        total[1:2, :], axis=1, keepdims=True
    )
    response = heat_response()

    @pl.when(is_ocean)
    def _():
        spread = jnp.zeros((8, 128), F32)
        for k in range(NSTEP):
            spread = jnp.where(row8 == k, response[k], spread)
        spread = spread * correction

        def body(x, carry):
            fp[NSTEP, x + 1, 0:8, :] = (
                fp[NSTEP, x + 1, 0:8, :] + spread * grid[4, pl.ds(x, 1), :]
            )
            return carry

        lax.fori_loop(0, CX, body, 0)

    stores = []
    for x in range(CX):
        copy = pltpu.make_async_copy(
            fp.at[NSTEP, x + 1, pl.ds(0, LEV), :], theta_out.at[0, :, x, :], lsem.at[8 + x]
        )
        copy.start()
        stores.append(copy)
    for s in range(NSTEP):
        drain_halo(s)
    for d, j, peer in export_peers:
        export_copy(d, j, peer).wait_send()
    for phase in range(phases):
        for j in range(len(sum_phases[phase])):
            sum_copy(phase, j).wait_send()
    loaded("surface")
    for copy in stores:
        copy.wait()


def solution(mesh):
    n_gx = mesh.shape["gx"]
    n_gy = mesh.shape["gy"]
    sources = 3 * n_gy
    phases = 1 + len(radices(n_gx))
    widest = max(2 * n_gy - 1, 3)
    constants = tables()

    def per_device(theta, surface, kappa, depth, wet, ids, counts, weights):
        spec = pl.BlockSpec(memory_space=pl.ANY)
        dma = pltpu.SemaphoreType.DMA
        return pl.pallas_call(
            functools.partial(kernel, n_gx, n_gy),
            out_shape=(
                jax.ShapeDtypeStruct((1, LEV, CX, CY), F32),
                jax.ShapeDtypeStruct((1, CX, CY), F32),
            ),
            in_specs=[spec] * 9,
            out_specs=(spec, spec),
            scratch_shapes=[
                pltpu.VMEM((NSTEP + 1, CX + 2, ROWS, CY), F32),
                pltpu.VMEM((NSTEP, 4, 8, CY), F32),
                pltpu.VMEM((NSTEP, 6, 4, 8, CY), F32),
                pltpu.VMEM((CX + 2, ROWS, CY), F32),
                pltpu.VMEM((2, CX, CY), F32),
                pltpu.VMEM((64, 128), F32),
                pltpu.VMEM((sources, 64, 128), F32),
                pltpu.VMEM((sources * 64, 256), BF16),
                pltpu.VMEM((8, 32, 16, 128), BF16),
                pltpu.VMEM((640, 256), BF16),
                pltpu.VMEM((8, 32, SLOTS), jnp.int32),
                pltpu.VMEM((8, 32), jnp.int32),
                pltpu.VMEM((CX, CY), jnp.int32),
                pltpu.VMEM((11, CX, CY), F32),
                pltpu.VMEM((4, 256, 128), BF16),
                pltpu.VMEM((2, 4, 8, 128), F32),
                pltpu.VMEM((2, CX, CY), F32),
                pltpu.VMEM((15, CX, CY), F32),
                pltpu.VMEM((14, CX, CY), F32),
                pltpu.VMEM((phases + 1, 8, 128), F32),
                pltpu.VMEM((phases, widest, 8, 128), F32),
                dma((42,)),
                dma((NSTEP, 8)),
                dma((NSTEP, 8)),
                dma((sources,)),
                dma((sources,)),
                dma((phases, widest)),
                dma((phases, widest)),
            ],
            compiler_params=pltpu.CompilerParams(
                collective_id=0, has_side_effects=True, vmem_limit_bytes=60 * 1024 * 1024
            ),
        )(theta, surface, kappa, depth, wet, ids, counts, weights, jnp.asarray(constants))

    in_specs = (
        P("comp", None, "gx", "gy"),
        P("comp", "gx", "gy"),
        P("comp", "gx", "gy"),
        P("gx", "gy"),
        P("gx", "gy"),
        P("comp", "gx", "gy", None),
        P("comp", "gx", "gy"),
        P("comp", "gx", "gy", None, None),
    )
    out_specs = (P("comp", None, "gx", "gy"), P("comp", "gx", "gy"))
    return jax.shard_map(
        per_device, mesh=mesh, in_specs=in_specs, out_specs=out_specs, check_vma=False
    )
```

profile of v0, /device:TPU:1, one launch (start us, length us, event | category | flops | bytes accessed | tf_op | source)
XLA Modules:
  0.0 97.2 jit_solution(4168424504951100006)
XLA Ops:
  0.6 1.5 %copy.11.ids = s32[1,8,32,8]{3,2,1,0:T(8,128)} copy(s32[1,8,32,8]{2,3,1,0:T(8,128)} %param.14) | data formatting | bytes 16384 | tf_op args[5]
  2.1 92.4 %shard_map.104 = (f32[1,48,32,128]{3,2,1,0:T(8,128)}, f32[1,32,128]{2,1,0:T(8,128)}) custom-call(f32[1,48,32,128]{3,2,1,0:T(8,128)} %theta.1, f32[1,32,128]{2,1,0:T(8,128)} %surface.1, f32[1,32,128]{2,1,0:T(8,128)} %kappa.1, f32[32,128]{1,0:T(8,128)} %depth.1, s32[32,128]{1,0:T(8,128)} %wet.1, s32[1,8,32,8]{3,2,1,0:T(8,128)} %copy.11.ids, ...), custom_call_target="tpu_custom_call" | custom-call | tf_op jit(solution)/shard_map/pallas_call | solution.py:773
  94.5 0.0 copy-start
  94.5 2.1 %copy.14 = f32[1,48,32,128]{3,2,1,0:T(8,128)} copy(f32[1,48,32,128]{3,2,1,0:T(8,128)} %get-tuple-element.4) | data formatting | bytes 1572864
  96.6 0.0 copy-done
  96.6 0.6 copy.15
Async XLA Ops:
  94.5 2.1 %copy-start = (f32[1,32,128]{2,1,0:T(8,128)S(1)}, f32[1,32,128]{2,1,0:T(8,128)}, u32[]{:S(2)}) copy-start(f32[1,32,128]{2,1,0:T(8,128)} %get-tuple-element.5) | copy-start | bytes 49156
where the time goes:
time: 98.5 us; the launch traced here: 97.2 us
  Pallas kernels  92.4 us (94%)
  local copies, waits for them, and re-layouts  4.19 us (4%)
    pallas_call x1, Pallas kernels, per_device(): pl.pallas_call(functools.partial(kernel, n_gx, n_gy), out_shape=(jax.Shap...  92.4 us
    unnamed x5, local copies, waits for them, and re-layouts  4.19 us

commit v1 on v0

--- a/solution.py
+++ b/solution.py
@@ -21,6 +21,10 @@
 CY = 128
 ROWS = 56
 SURF = 48
+PACK = 32
+UNPACK = 32
+OCEAN = 16
+AIR = 4
 
 node_derivative = np.array(
     [
@@ -243,7 +247,7 @@
             return tuple(accs)
 
         zero = jnp.zeros((8, 128), F32)
-        accs = lax.fori_loop(0, CX, body, (zero,) * 4)
+        accs = lax.fori_loop(0, CX, body, (zero,) * 4, unroll=PACK)
         for j in range(4):
             ys[s, j] = accs[j]
 
@@ -310,7 +314,7 @@
             fill(x, own, x + 1)
             return carry
 
-        lax.fori_loop(0, CX, body, 0)
+        lax.fori_loop(0, CX, body, 0, unroll=UNPACK)
         if corners:
             fill(CX - 1, merged(s, 2, 4), 0)
             fill(0, merged(s, 3, 5), CX + 1)
@@ -479,7 +483,7 @@
                 fp[s, x + 1, 0:1, :] = new[0:1, :] + grid[7, pl.ds(x, 1), :]
             return carry
 
-        lax.fori_loop(0, CX, body, 0)
+        lax.fori_loop(0, CX, body, 0, unroll=OCEAN)
 
     def air_step(s):
         h = jnp.where(
@@ -539,7 +543,7 @@
                         )
             return carry
 
-        lax.fori_loop(0, CX // 4, body, 0)
+        lax.fori_loop(0, CX // 4, body, 0, unroll=AIR)
 
     def forward(s):
         @pl.when(is_ocean)
@@ -691,10 +695,10 @@
         if s - 2 >= 1 and s - 2 < phases:
             sum_send(s - 2)
         wait_halo(s - 1)
+        unpack(s - 1, True)
+        forward(s)
         if s - 2 < phases:
             sum_finish(s - 2)
-        unpack(s - 1, True)
-        forward(s)
         if s <= ITERS:
             recurrence_next = 1.0 / (2.0 * spread_ratio - recurrence)
 

time: 98.5 us -> 68 us (0.69); the launches traced: 97.2 us -> 67.8 us
  Pallas kernels: 92.4 us -> 63 us
    pallas_call x1, Pallas kernels: 92.4 us -> 63 us  [per_device(): pl.pallas_call(functools.partial(kernel, n_gx, n_gy), out_shape=(jax.Shap...]
where the time goes in v1:
time: 68 us; the launch traced here: 67.8 us
  Pallas kernels  63 us (93%)
  local copies, waits for them, and re-layouts  4.19 us (6%)
    pallas_call x1, Pallas kernels, per_device(): pl.pallas_call(functools.partial(kernel, n_gx, n_gy), out_shape=(jax.Shap...  63 us
    unnamed x5, local copies, waits for them, and re-layouts  4.19 us

profile of v1, /device:TPU:1, one launch (start us, length us, event | category | flops | bytes accessed | tf_op | source)
XLA Modules:
  0.0 67.8 jit_solution(6760118133857300981)
XLA Ops:
  0.6 1.5 %copy.11.ids = s32[1,8,32,8]{3,2,1,0:T(8,128)} copy(s32[1,8,32,8]{2,3,1,0:T(8,128)} %param.14) | data formatting | bytes 16384 | tf_op args[5]
  2.1 63.0 %shard_map.104 = (f32[1,48,32,128]{3,2,1,0:T(8,128)}, f32[1,32,128]{2,1,0:T(8,128)}) custom-call(f32[1,48,32,128]{3,2,1,0:T(8,128)} %theta.1, f32[1,32,128]{2,1,0:T(8,128)} %surface.1, f32[1,32,128]{2,1,0:T(8,128)} %kappa.1, f32[32,128]{1,0:T(8,128)} %depth.1, s32[32,128]{1,0:T(8,128)} %wet.1, s32[1,8,32,8]{3,2,1,0:T(8,128)} %copy.11.ids, ...), custom_call_target="tpu_custom_call" | custom-call | tf_op jit(solution)/shard_map/pallas_call | solution.py:777
  65.1 0.0 copy-start
  65.1 2.1 %copy.14 = f32[1,48,32,128]{3,2,1,0:T(8,128)} copy(f32[1,48,32,128]{3,2,1,0:T(8,128)} %get-tuple-element.4) | data formatting | bytes 1572864
  67.2 0.0 copy-done
  67.2 0.6 copy.15
Async XLA Ops:
  65.1 2.1 %copy-start = (f32[1,32,128]{2,1,0:T(8,128)S(1)}, f32[1,32,128]{2,1,0:T(8,128)}, u32[]{:S(2)}) copy-start(f32[1,32,128]{2,1,0:T(8,128)} %get-tuple-element.5) | copy-start | bytes 49156

commit v2 on v0

--- a/solution.py
+++ b/solution.py
@@ -21,6 +21,8 @@
 CY = 128
 ROWS = 56
 SURF = 48
+EDGE = (0, 1, 2, 3, 28, 29, 30, 31)
+INNER = tuple(range(4, 28))
 
 node_derivative = np.array(
     [
@@ -116,6 +118,8 @@
     fp,
     ys,
     yr,
+    ye,
+    yer,
     zb,
     ex,
     tsend,
@@ -231,29 +235,74 @@
         fp[0, x + 1, SURF + 3 : SURF + 4, :] = grid[4, x : x + 1, :]
         fp[0, x + 1, SURF + 4 : SURF + 8, :] = jnp.zeros((4, 128), F32)
 
-    def pack(s):
-        def body(x, accs):
-            accs = list(accs)
-            for b in range(7):
-                base = 2 * x + 64 * (b % 2)
-                moved = pltpu.roll(fp[s, x + 1, 8 * b : 8 * b + 8, :], base + 1, 1)
-                accs[b // 2] = jnp.where(
-                    (lane128 == base) | (lane128 == base + 1), moved, accs[b // 2]
-                )
-            return tuple(accs)
-
-        zero = jnp.zeros((8, 128), F32)
-        accs = lax.fori_loop(0, CX, body, (zero,) * 4)
+    def place_in(acc, moved, lane):
+        return jnp.where((lane128 == lane) | (lane128 == lane + 1), moved, acc)
+
+    def pack_inner(s, slabs, blocks):
         for j in range(4):
-            ys[s, j] = accs[j]
+            acc = jnp.zeros((8, 128), F32)
+            found = False
+            for b in (2 * j, 2 * j + 1):
+                if b in blocks:
+                    found = True
+                    for x in slabs:
+                        lane = 2 * x + 64 * (b % 2)
+                        moved = pltpu.roll(fp[s, x + 1, 8 * b : 8 * b + 8, :], (lane + 1) % 128, 1)
+                        acc = place_in(acc, moved, lane)
+            if found:
+                ys[s, j] = acc
+
+    def pack_edge(s, blocks):
+        acc = jnp.zeros((8, 128), F32)
+        for b in blocks:
+            for e, x in enumerate(EDGE):
+                lane = 16 * b + 2 * e
+                moved = pltpu.roll(fp[s, x + 1, 8 * b : 8 * b + 8, :], lane + 1, 1)
+                acc = place_in(acc, moved, lane)
+        ye[s] = acc
+
+    def merge(low, high):
+        return jnp.where(lane128 % 2 == 0, low, pltpu.roll(high, 126, 1))
+
+    def turn(value, lane):
+        return pltpu.roll(value, (128 - lane) % 128, 1) if lane % 128 else value
+
+    def unpack_inner(s, slabs, blocks):
+        for j in range(4):
+            if 2 * j in blocks or 2 * j + 1 in blocks:
+                both = merge(yr[s, 0, j], yr[s, 1, j])
+                for b in (2 * j, 2 * j + 1):
+                    if b in blocks:
+                        for x in slabs:
+                            zb[x + 1, 8 * b : 8 * b + 8, :] = turn(both, 2 * x + 64 * (b % 2))
+
+    def unpack_edge(s, blocks):
+        both = merge(yer[s, 0], yer[s, 1])
+        for b in blocks:
+            for e, x in enumerate(EDGE):
+                zb[x + 1, 8 * b : 8 * b + 8, :] = turn(both, 16 * b + 2 * e)
+
+    def unpack_corner(s, blocks):
+        west = merge(yer[s, 2], yer[s, 4])
+        east = merge(yer[s, 3], yer[s, 5])
+        for b in blocks:
+            zb[0, 8 * b : 8 * b + 8, :] = turn(west, 16 * b + 14)
+            zb[CX + 1, 8 * b : 8 * b + 8, :] = turn(east, 16 * b)
 
     def copy_to(s, d):
-        if d == 0:
-            src, dst, peer = fp.at[s, CX], fp.at[s, 0], halo_peers[0]
-        elif d == 1:
-            src, dst, peer = fp.at[s, 1], fp.at[s, CX + 1], halo_peers[1]
+        peer = halo_peers[d % 2 if d < 4 else 2 + d % 2 if d < 10 else d - 6]
+        if d < 4:
+            rows = pl.ds(0, LEV) if d < 2 else pl.ds(SURF, 8)
+            src = fp.at[s, CX if d % 2 == 0 else 1, rows, :]
+            dst = fp.at[s, 0 if d % 2 == 0 else CX + 1, rows, :]
+        elif d < 6:
+            src, dst = ye.at[s], yer.at[s, d - 4]
+        elif d < 8:
+            src, dst = ys.at[s, pl.ds(0, 3)], yr.at[s, d - 6, pl.ds(0, 3)]
+        elif d < 10:
+            src, dst = ys.at[s, 3], yr.at[s, d - 8, 3]
         else:
-            src, dst, peer = ys.at[s], yr.at[s, d - 2], halo_peers[d]
+            src, dst = ye.at[s], yer.at[s, d - 8]
         return pltpu.make_async_remote_copy(
             src_ref=src,
             dst_ref=dst,
@@ -263,57 +312,31 @@
             device_id_type=MESH,
         )
 
-    def send_halo(s):
-        for d in range(4):
-            copy_to(s, d).start()
+    SLAB, SLAB_SURF, OUTER, INSIDE, SURF_COLUMN = (0, 1), (2, 3), (4, 5), (6, 7), (8, 9)
+    CORNER = (10, 11, 12, 13)
+
+    def send(s, *kinds):
+        for kind in kinds:
+            for d in kind:
+                copy_to(s, d).start()
+
+    def wait(s, *kinds):
+        for kind in kinds:
+            for d in kind:
+                copy_to(s, d).wait_recv()
+
+    def drain_halo(s):
+        kinds = [SLAB, OUTER, INSIDE]
+        if s < ITERS:
+            kinds += [SLAB_SURF, SURF_COLUMN]
+        for kind in kinds:
+            for d in kind:
+                copy_to(s, d).wait_send()
 
         @pl.when(is_air)
         def _():
-            for d in range(4, 8):
-                copy_to(s, d).start()
-
-    def wait_halo(s):
-        for d in range(4):
-            copy_to(s, d).wait_recv()
-
-        @pl.when(is_air)
-        def _():
-            for d in range(4, 8):
-                copy_to(s, d).wait_recv()
-
-    def drain_halo(s):
-        for d in range(4):
-            copy_to(s, d).wait_send()
-
-        @pl.when(is_air)
-        def _():
-            for d in range(4, 8):
+            for d in CORNER:
                 copy_to(s, d).wait_send()
-
-    def merged(s, south, north):
-        found = []
-        for j in range(4):
-            low = yr[s, south, j]
-            high = pltpu.roll(yr[s, north, j], 126, 1)
-            found.append(jnp.where(lane128 % 2 == 0, low, high))
-        return found
-
-    def unpack(s, corners):
-        own = merged(s, 0, 1)
-
-        def fill(x, vectors, slab):
-            for b in range(7):
-                shift = lax.rem(256 - 2 * x - 64 * (b % 2), 128)
-                zb[slab, 8 * b : 8 * b + 8, :] = pltpu.roll(vectors[b // 2], shift, 1)
-
-        def body(x, carry):
-            fill(x, own, x + 1)
-            return carry
-
-        lax.fori_loop(0, CX, body, 0)
-        if corners:
-            fill(CX - 1, merged(s, 2, 4), 0)
-            fill(0, merged(s, 3, 5), CX + 1)
 
     def export_copy(d, j, peer):
         slot = (1 - d) * n_gy + gy
@@ -326,43 +349,71 @@
             device_id_type=MESH,
         )
 
-    loaded("theta")
-    pack(0)
+    ALL = tuple(range(CX))
+    LEVELS = tuple(range(6))
+    BOTH = tuple(range(7))
     pl.semaphore_wait(barrier, len(greeted))
     for d, j, peer in export_peers:
         export_copy(d, j, peer).start()
-    send_halo(0)
+    loaded("theta")
+    send(0, SLAB, SLAB_SURF)
+    pack_edge(0, BOTH)
+    send(0, OUTER)
+
+    @pl.when(is_air)
+    def _():
+        send(0, CORNER)
+
+    pack_inner(0, INNER, LEVELS)
+    pack_inner(0, ALL, (6,))
+    send(0, INSIDE, SURF_COLUMN)
 
     loaded("remap")
     loaded("tables")
-    cnt = cntbuf[...].astype(F32)
-    lane32 = lax.broadcasted_iota(jnp.int32, (32, 32), 1)
-    row32 = lax.broadcasted_iota(jnp.int32, (32, 32), 0)
-    ones = jnp.ones((32, 128), BF16)
-    counted = []
+    gy_bits = n_gy.bit_length() - 1
+    id_all = idbuf[...]
+    unit = id_all & (units - 1)
+    dev = id_all >> 8
+    dev_gy = dev & (n_gy - 1)
+    offset = (dev >> gy_bits) - gx + 1
+    offset = jnp.where(offset < 0, offset + n_gx, jnp.where(offset >= n_gx, offset - n_gx, offset))
+    tile_y = unit & 31
+    source = offset * n_gy + dev_gy
+    row = (tile_y >> 2) * 8 + (unit >> 5)
+    low_tile = tile_y & 3
+    slot_order = lax.broadcasted_iota(jnp.int32, (8, SLOTS, 32), 1)
+    source = jnp.where(slot_order < cntbuf[...][:, None, :], source, 200)
+    eye = jnp.where(
+        lax.broadcasted_iota(jnp.int32, (32, 32), 0) == lax.broadcasted_iota(jnp.int32, (32, 32), 1),
+        1.0,
+        0.0,
+    ).astype(BF16)
+    columns = []
     for tx in range(8):
-        spread = jnp.where(lane32 == row32, jnp.broadcast_to(cnt[tx : tx + 1, :], (32, 32)), 0.0)
-        counted.append(dot(spread.astype(BF16), ones)[:, :SLOTS])
-    counted = jnp.concatenate(counted, axis=0)
-    id_all = idbuf[...].reshape(units, SLOTS)
-    slot_lane = lax.broadcasted_iota(jnp.int32, (units, SLOTS), 1)
-    dev = id_all // units
-    unit = id_all - dev * units
-    dev_gx = dev // n_gy
-    dev_gy = dev - dev_gx * n_gy
-    tile_x = unit // 32
-    tile_y = unit - tile_x * 32
-    offset = dev_gx - gx + 1
-    offset = jnp.where(offset < 0, offset + n_gx, jnp.where(offset >= n_gx, offset - n_gx, offset))
-    key = (offset * n_gy + dev_gy) * 64 + (tile_y // 4) * 8 + tile_x
-    key = jnp.where(slot_lane.astype(F32) < counted, key, -1)
-    tile_low = tile_y - (tile_y // 4) * 4
-
-    wait_halo(0)
-    unpack(0, True)
-
-    def rims(s, row):
-        pass
+        stacked = jnp.concatenate([source[tx], row[tx], low_tile[tx], low_tile[tx]], axis=0)
+        columns.append(
+            lax.dot_general(
+                eye,
+                stacked.astype(F32).astype(BF16),
+                (((1,), (1,)), ((), ())),
+                preferred_element_type=F32,
+            )
+        )
+    columns = jnp.concatenate(columns, axis=0)
+    key = columns[:, 0:8] * 64.0 + columns[:, 8:16]
+    tile_low = columns[:, 16:24]
+
+    wait(0, INSIDE, OUTER, SURF_COLUMN)
+    unpack_inner(0, INNER, LEVELS)
+    unpack_inner(0, ALL, (6,))
+    unpack_edge(0, LEVELS)
+    wait(0, SLAB, SLAB_SURF)
+
+    @pl.when(is_air)
+    def _():
+        wait(0, CORNER)
+        unpack_corner(0, BOTH)
+
 
     def lanes_of(shape):
         return lax.broadcasted_iota(jnp.int32, shape, 1)
@@ -447,20 +498,18 @@
             index += 2
         return values * pcr[14]
 
-    lane56 = lanes_of((ROWS, CY))
-    row56 = lax.broadcasted_iota(jnp.int32, (ROWS, CY), 0)
     row48 = lax.broadcasted_iota(jnp.int32, (LEV, CY), 0)
     lane48 = lanes_of((LEV, CY))
 
-    def ocean_step(s):
-        def body(x, carry):
+    def ocean_step(s, slabs):
+        for x in slabs:
             c = fp[s - 1, x + 1, 0:LEV, :]
             w = fp[s - 1, x, 0:LEV, :]
             e = fp[s - 1, x + 2, 0:LEV, :]
             z = zb[x + 1, 0:LEV, :]
 
-            def row(i):
-                return coef[i, pl.ds(x, 1), :]
+            def row(i, x=x):
+                return coef[i, x : x + 1, :]
 
             n = jnp.where(lane48 == CY - 1, z, pltpu.roll(c, CY - 1, 1))
             o = jnp.where(lane48 == 0, z, pltpu.roll(c, 1, 1))
@@ -476,81 +525,77 @@
             )
             fp[s, x + 1, 0:LEV, :] = new
             if s > 1:
-                fp[s, x + 1, 0:1, :] = new[0:1, :] + grid[7, pl.ds(x, 1), :]
-            return carry
-
-        lax.fori_loop(0, CX, body, 0)
-
-    def air_step(s):
+                fp[s, x + 1, 0:1, :] = new[0:1, :] + grid[7, x : x + 1, :]
+
+    def air_step(s, tiles):
+        rows = ROWS if s <= ITERS else LEV
+        lane_r = lanes_of((rows, CY))
+        row_r = lax.broadcasted_iota(jnp.int32, (rows, CY), 0)
         h = jnp.where(
             ((lane1 % 4 == 0) & ((lane1 > 0) | has_south))
             | ((lane1 % 4 == 3) & ((lane1 < CY - 1) | has_north)),
             0.5,
             0.0,
         )
-        mix_up = jnp.where(row56 < LEV - 1, vertical_mix, 0.0)
-        mix_down = jnp.where((row56 > 0) & (row56 < LEV), vertical_mix, 0.0)
-
-        def body(i, carry):
+        mix_up = jnp.where(row_r < LEV - 1, vertical_mix, 0.0)
+        mix_down = jnp.where((row_r > 0) & (row_r < LEV), vertical_mix, 0.0)
+
+        for i in tiles:
             x0 = 4 * i
-            v = [fp[s - 1, x0 + j] for j in range(6)]
-            z = [zb[x0 + j] for j in range(6)]
+            v = [fp[s - 1, x0 + j, 0:rows, :] for j in range(6)]
+            z = [zb[x0 + j, 0:rows, :] for j in range(6)]
 
             def across(t):
                 return [0.5 * (t[1] + t[0]), t[2], t[3], 0.5 * (t[4] + t[5])]
 
             blocks = []
             for a, za in zip(across(v), across(z)):
-                partner = jnp.where(lane56 % 4 == 0, pltpu.roll(a, 1, 1), pltpu.roll(a, CY - 1, 1))
-                partner = jnp.where((lane56 == 0) | (lane56 == CY - 1), za, partner)
+                partner = jnp.where(lane_r % 4 == 0, pltpu.roll(a, 1, 1), pltpu.roll(a, CY - 1, 1))
+                partner = jnp.where((lane_r == 0) | (lane_r == CY - 1), za, partner)
                 blocks.append(a + h * (partner - a))
             high, low = split(jnp.concatenate(blocks, axis=0))
             along = dot(jnp.concatenate([high, low], axis=1), cbuf[256:512, :])
             along = along[:, :CY] + along[:, CY:]
             for j in range(4):
                 b = blocks[j]
-                lap = along[ROWS * j : ROWS * (j + 1)]
+                lap = along[rows * j : rows * (j + 1)]
                 for m in range(4):
                     lap = lap + float(second_derivative[j, m]) * blocks[m]
-                up = pltpu.roll(b, ROWS - 1, 0)
+                up = pltpu.roll(b, rows - 1, 0)
                 down = pltpu.roll(b, 1, 0)
                 new = (
                     b
-                    + grid[2, pl.ds(x0 + j, 1), :] * lap
+                    + grid[2, x0 + j : x0 + j + 1, :] * lap
                     + mix_up * (up - b)
                     + mix_down * (down - b)
                 )
                 x = x0 + j
-                fp[s, x + 1] = new
+                fp[s, x + 1, 0:rows, :] = new
                 if s == 1:
-                    grid[8, pl.ds(x, 1), :] = b[0:1, :]
-                    grid[9, pl.ds(x, 1), :] = b[SURF : SURF + 1, :]
+                    grid[8, x : x + 1, :] = b[0:1, :]
+                    grid[9, x : x + 1, :] = b[SURF : SURF + 1, :]
                 else:
                     fp[s, x + 1, 0:1, :] = (
                         new[0:1, :]
-                        + grid[6, pl.ds(x, 1), :]
-                        - grid[7, pl.ds(x, 1), :] * b[0:1, :]
+                        + grid[6, x : x + 1, :]
+                        - grid[7, x : x + 1, :] * b[0:1, :]
                     )
                     if s <= ITERS:
                         fp[s, x + 1, SURF : SURF + 1, :] = (
                             new[SURF : SURF + 1, :]
-                            + grid[10, pl.ds(x, 1), :]
+                            + grid[10, x : x + 1, :]
                             - press_rate * b[SURF : SURF + 1, :]
                         )
-            return carry
-
-        lax.fori_loop(0, CX // 4, body, 0)
-
-    def forward(s):
-        @pl.when(is_ocean)
-        def _():
-            ocean_step(s)
-
-        @pl.when(is_air)
-        def _():
-            air_step(s)
-
-    forward(1)
+
+
+    @pl.when(is_ocean)
+    def _():
+        ocean_step(1, ALL)
+
+    @pl.when(is_air)
+    def _():
+        unpack_edge(0, (6,))
+        air_step(1, tuple(range(CX // 4)))
 
     for d in range(3):
         for j in range(n_gy):
@@ -566,9 +611,9 @@
     high, low = split(trecv[...].reshape(sources * 64, 128))
     table[:, 0:128] = high
     table[:, 128:256] = low
-    key_lane = lax.broadcasted_iota(jnp.int32, (units, sources * 64), 1)
+    key_lane = lax.broadcasted_iota(jnp.int32, (units, sources * 64), 1).astype(F32)
     lane256 = lax.broadcasted_iota(jnp.int32, (units, 256), 1)
-    low_lane = (lane256 // 4) % 4
+    low_lane = ((lane256 // 4) % 4).astype(F32)
     slot_of = (lane256 // 16) % 8
     picked = jnp.zeros((units, 256), F32)
     for m in range(SLOTS):
@@ -654,8 +699,9 @@
 
     def put_surface(s, value):
         grid[13] = value
-        for x in range(CX):
-            fp[s, x + 1, SURF : SURF + 1, :] = grid[13, x : x + 1, :]
+        if s < ITERS:
+            for x in range(CX):
+                fp[s, x + 1, SURF : SURF + 1, :] = grid[13, x : x + 1, :]
 
     @pl.when(is_ocean)
     def _():
@@ -663,12 +709,20 @@
         grid[7] = force
         for x in range(CX):
             fp[1, x + 1, 0:1, :] = fp[1, x + 1, 0:1, :] + grid[7, x : x + 1, :]
+        send(1, SLAB)
+        pack_edge(1, LEVELS)
+        send(1, OUTER)
+        pack_inner(1, INNER, LEVELS)
+        send(1, INSIDE)
         eta = grid[1]
         residual = wet_c * (damping * eta + fresh_rate * imp[1]) - apply_a(0, eta)
         direction = solve(residual) / centre
         grid[11] = eta + direction
         grid[12] = residual
         put_surface(1, direction)
+        send(1, SLAB_SURF)
+        pack_inner(1, ALL, (6,))
+        send(1, SURF_COLUMN)
 
     @pl.when(is_air)
     def _():
@@ -682,24 +736,29 @@
             fp[1, x + 1, SURF : SURF + 1, :] = (
                 fp[1, x + 1, SURF : SURF + 1, :] + grid[11, x : x + 1, :]
             )
+        send(1, SLAB, SLAB_SURF)
+        pack_edge(1, BOTH)
+        send(1, CORNER, OUTER)
+        pack_inner(1, INNER, BOTH)
+        send(1, INSIDE, SURF_COLUMN)
 
     recurrence = 1.0 / spread_ratio
     phases = len(sum_phases)
     for s in range(2, NSTEP + 1):
-        pack(s - 1)
-        send_halo(s - 1)
-        if s - 2 >= 1 and s - 2 < phases:
-            sum_send(s - 2)
-        wait_halo(s - 1)
-        if s - 2 < phases:
-            sum_finish(s - 2)
-        unpack(s - 1, True)
-        forward(s)
-        if s <= ITERS:
-            recurrence_next = 1.0 / (2.0 * spread_ratio - recurrence)
-
-            @pl.when(is_ocean)
-            def _(s=s, recurrence=recurrence, recurrence_next=recurrence_next):
+        last = s == NSTEP
+        recurrence_next = 1.0 / (2.0 * spread_ratio - recurrence)
+
+        @pl.when(is_ocean)
+        def _(s=s, last=last, recurrence=recurrence, recurrence_next=recurrence_next):
+            wait(s - 1, INSIDE)
+            unpack_inner(s - 1, INNER, LEVELS)
+            ocean_step(s, INNER)
+            if not last:
+                pack_inner(s, INNER, LEVELS)
+                send(s, INSIDE)
+            if s <= ITERS:
+                wait(s - 1, SURF_COLUMN, SLAB_SURF)
+                unpack_inner(s - 1, ALL, (6,))
                 old = grid[13]
                 residual = grid[12] - apply_a(s - 1, old)
                 direction = (recurrence_next * recurrence) * old + (
@@ -708,16 +767,56 @@
                 grid[11] = grid[11] + direction
                 grid[12] = residual
                 put_surface(s, direction)
-
-            recurrence = recurrence_next
+                if s < ITERS:
+                    send(s, SLAB_SURF)
+                    pack_inner(s, ALL, (6,))
+                    send(s, SURF_COLUMN)
+            wait(s - 1, OUTER, SLAB)
+            unpack_edge(s - 1, LEVELS)
+            ocean_step(s, EDGE)
+            if not last:
+                send(s, SLAB)
+                pack_edge(s, LEVELS)
+                send(s, OUTER)
+
+        @pl.when(is_air)
+        def _(s=s, last=last):
+            used = BOTH if s <= ITERS else LEVELS
+            made = BOTH if s < ITERS else LEVELS
+            wait(s - 1, INSIDE, OUTER)
+            if s <= ITERS:
+                wait(s - 1, SURF_COLUMN)
+            unpack_inner(s - 1, INNER, used)
+            unpack_edge(s - 1, used)
+            air_step(s, tuple(range(1, CX // 4 - 1)))
+            if not last:
+                pack_inner(s, INNER, made)
+                send(s, INSIDE)
+                if s < ITERS:
+                    send(s, SURF_COLUMN)
+            wait(s - 1, SLAB, CORNER)
+            if s <= ITERS:
+                wait(s - 1, SLAB_SURF)
+            unpack_corner(s - 1, used)
+            air_step(s, (0, CX // 4 - 1))
+            if not last:
+                send(s, SLAB)
+                if s < ITERS:
+                    send(s, SLAB_SURF)
+                pack_edge(s, made)
+                send(s, CORNER, OUTER)
+            if s == ITERS:
+                gather_row(s, SURF, 11)
+
+        recurrence = recurrence_next
         if s == ITERS:
-
-            @pl.when(is_air)
-            def _(s=s):
-                gather_row(s, SURF, 11)
-
             loads["surface"] = [pltpu.make_async_copy(grid.at[11], surface_out.at[0], lsem.at[41])]
             loads["surface"][0].start()
+        phase = s - 2
+        if phase < phases:
+            sum_finish(phase)
+            if phase + 1 < phases:
+                sum_send(phase + 1)
 
     total = red[phases]
     correction = jnp.sum(total[0:1, :], axis=1, keepdims=True) / jnp.sum(
@@ -781,7 +880,9 @@
             scratch_shapes=[
                 pltpu.VMEM((NSTEP + 1, CX + 2, ROWS, CY), F32),
                 pltpu.VMEM((NSTEP, 4, 8, CY), F32),
-                pltpu.VMEM((NSTEP, 6, 4, 8, CY), F32),
+                pltpu.VMEM((NSTEP, 2, 4, 8, CY), F32),
+                pltpu.VMEM((NSTEP, 8, CY), F32),
+                pltpu.VMEM((NSTEP, 6, 8, CY), F32),
                 pltpu.VMEM((CX + 2, ROWS, CY), F32),
                 pltpu.VMEM((2, CX, CY), F32),
                 pltpu.VMEM((64, 128), F32),
@@ -789,7 +890,7 @@
                 pltpu.VMEM((sources * 64, 256), BF16),
                 pltpu.VMEM((8, 32, 16, 128), BF16),
                 pltpu.VMEM((640, 256), BF16),
-                pltpu.VMEM((8, 32, SLOTS), jnp.int32),
+                pltpu.VMEM((8, SLOTS, 32), jnp.int32),
                 pltpu.VMEM((8, 32), jnp.int32),
                 pltpu.VMEM((CX, CY), jnp.int32),
                 pltpu.VMEM((11, CX, CY), F32),
@@ -801,8 +902,8 @@
                 pltpu.VMEM((phases + 1, 8, 128), F32),
                 pltpu.VMEM((phases, widest, 8, 128), F32),
                 dma((42,)),
-                dma((NSTEP, 8)),
-                dma((NSTEP, 8)),
+                dma((NSTEP, 14)),
+                dma((NSTEP, 14)),
                 dma((sources,)),
                 dma((sources,)),
                 dma((phases, widest)),
@@ -811,7 +912,17 @@
             compiler_params=pltpu.CompilerParams(
                 collective_id=0, has_side_effects=True, vmem_limit_bytes=60 * 1024 * 1024
             ),
-        )(theta, surface, kappa, depth, wet, ids, counts, weights, jnp.asarray(constants))
+        )(
+            theta,
+            surface,
+            kappa,
+            depth,
+            wet,
+            ids.transpose(0, 1, 3, 2),
+            counts,
+            weights,
+            jnp.asarray(constants),
+        )
 
     in_specs = (
         P("comp", None, "gx", "gy"),

time: 98.5 us -> 57.4 us (0.58); the launches traced: 97.2 us -> 57.3 us
  Pallas kernels: 92.4 us -> 53.9 us
  local copies, waits for them, and re-layouts: 4.19 us -> 2.68 us
    pallas_call x1, Pallas kernels: 92.4 us -> 53.9 us  [per_device(): pl.pallas_call(functools.partial(kernel, n_gx, n_gy), out_shape=(jax.Shap...]
    unnamed x5 -> x4, local copies, waits for them, and re-layouts: 4.19 us -> 2.68 us
where the time goes in v2:
time: 57.4 us; the launch traced here: 57.3 us
  Pallas kernels  53.9 us (94%)
  local copies, waits for them, and re-layouts  2.68 us (5%)
  between operations  0.65 us (1%)
    pallas_call x1, Pallas kernels, per_device(): pl.pallas_call(functools.partial(kernel, n_gx, n_gy), out_shape=(jax.Shap...  53.9 us
    unnamed x4, local copies, waits for them, and re-layouts  2.68 us

profile of v2, /device:TPU:1, one launch (start us, length us, event | category | flops | bytes accessed | tf_op | source)
XLA Modules:
  0.0 57.3 jit_solution(3150694562790431593)
XLA Ops:
  0.6 53.9 %shard_map.104 = (f32[1,48,32,128]{3,2,1,0:T(8,128)}, f32[1,32,128]{2,1,0:T(8,128)}) custom-call(f32[1,48,32,128]{3,2,1,0:T(8,128)} %theta.1, f32[1,32,128]{2,1,0:T(8,128)} %surface.1, f32[1,32,128]{2,1,0:T(8,128)} %kappa.1, f32[32,128]{1,0:T(8,128)} %depth.1, s32[32,128]{1,0:T(8,128)} %wet.1, s32[1,8,8,32]{3,2,1,0:T(8,128)} %bitcast.1, s32[1,8,32]{2,1,0:T(8,128)} %counts.1, ...), custom_call_target="tpu_custom_call" | custom-call | tf_op jit(solution)/shard_map/pallas_call | solution.py:872
  54.6 0.0 copy-start
  54.6 2.1 %copy.13 = f32[1,48,32,128]{3,2,1,0:T(8,128)} copy(f32[1,48,32,128]{3,2,1,0:T(8,128)} %get-tuple-element.4) | data formatting | bytes 1572864
  56.7 0.0 copy-done
  56.7 0.6 %copy.14 = f32[1,32,128]{2,1,0:T(8,128)} copy(f32[1,32,128]{2,1,0:T(8,128)S(1)} %copy-done) | data formatting | bytes 32768
Async XLA Ops:
  54.6 2.1 %copy-start = (f32[1,32,128]{2,1,0:T(8,128)S(1)}, f32[1,32,128]{2,1,0:T(8,128)}, u32[]{:S(2)}) copy-start(f32[1,32,128]{2,1,0:T(8,128)} %get-tuple-element.5) | copy-start | bytes 49156

commit v3 on v2

--- a/solution.py
+++ b/solution.py
@@ -113,8 +113,8 @@
     counts,
     weights,
     consts,
-    theta_out,
-    surface_out,
+    fin,
+    surface_fin,
     fp,
     ys,
     yr,
@@ -132,6 +132,7 @@
     wetbuf,
     coef,
     pb,
+    hot,
     dbuf,
     imp,
     pcr,
@@ -181,6 +182,11 @@
         sum_phases.append(group)
         stride *= size
 
+    barrier = pltpu.get_barrier_semaphore()
+    greeted = halo_peers + [p for _, _, p in export_peers] + [p for g in sum_phases for p in g]
+    for peer in greeted:
+        pl.semaphore_signal(barrier, inc=1, device_id=peer, device_id_type=MESH)
+
     loads = {}
 
     def load(name, index, src, dst):
@@ -203,11 +209,6 @@
     load("remap", 6, counts.at[0], cntbuf)
     load("tables", 7, consts, cbuf)
     load("weights", 40, weights.at[0], wbuf)
-
-    barrier = pltpu.get_barrier_semaphore()
-    greeted = halo_peers + [p for _, _, p in export_peers] + [p for g in sum_phases for p in g]
-    for peer in greeted:
-        pl.semaphore_signal(barrier, inc=1, device_id=peer, device_id_type=MESH)
 
     lane128 = lax.broadcasted_iota(jnp.int32, (8, 128), 1)
     lane1 = lax.broadcasted_iota(jnp.int32, (1, 128), 1)
@@ -352,21 +353,24 @@
     ALL = tuple(range(CX))
     LEVELS = tuple(range(6))
     BOTH = tuple(range(7))
+    loaded("theta")
+    pack_edge(0, BOTH)
+    pack_inner(0, INNER, LEVELS)
+    pack_inner(0, ALL, (6,))
     pl.semaphore_wait(barrier, len(greeted))
-    for d, j, peer in export_peers:
-        export_copy(d, j, peer).start()
-    loaded("theta")
-    send(0, SLAB, SLAB_SURF)
-    pack_edge(0, BOTH)
-    send(0, OUTER)
+    send(0, SLAB, SLAB_SURF, OUTER)
 
     @pl.when(is_air)
     def _():
         send(0, CORNER)
 
-    pack_inner(0, INNER, LEVELS)
-    pack_inner(0, ALL, (6,))
     send(0, INSIDE, SURF_COLUMN)
+    for d, j, peer in export_peers:
+        if d:
+            export_copy(d, j, peer).start()
+    for d, j, peer in export_peers:
+        if not d:
+            export_copy(d, j, peer).start()
 
     loaded("remap")
     loaded("tables")
@@ -402,6 +406,9 @@
     columns = jnp.concatenate(columns, axis=0)
     key = columns[:, 0:8] * 64.0 + columns[:, 8:16]
     tile_low = columns[:, 16:24]
+    key_lane = lax.broadcasted_iota(jnp.int32, (units, sources * 64), 1).astype(F32)
+    for m in range(SLOTS):
+        hot[m] = jnp.where(key[:, m : m + 1] == key_lane, 1.0, 0.0).astype(BF16)
 
     wait(0, INSIDE, OUTER, SURF_COLUMN)
     unpack_inner(0, INNER, LEVELS)
@@ -439,26 +446,37 @@
     def side_rows(s, row):
         return fp[s, 0, row : row + 1, :], fp[s, CX + 1, row : row + 1, :]
 
-    @pl.when(is_ocean)
-    def _():
+    def wet_sides():
         wet_c = grid[4]
         rim_row(SURF + 3, 5)
         we, ww, wn, ws = shifted(wet_c, *side_rows(0, SURF + 3), grid[5])
         wn = jnp.where((lane_full == CY - 1) & jnp.logical_not(has_north), 0.0, wn)
         ws = jnp.where((lane_full == 0) & jnp.logical_not(has_south), 0.0, ws)
-        for row, slot, at in ((SURF + 1, 2, 0), (SURF + 2, 3, 6)):
-            center = grid[slot]
-            rim_row(row, 5)
-            ke, kw, kn, ks = shifted(center, *side_rows(0, row), grid[5])
-            base = center * wet_c
-            coef[at] = 0.5 * (base + ke * we) * wet_c * we
-            coef[at + 1] = 0.5 * (kw * ww + base) * ww * wet_c
-            coef[at + 2] = 0.5 * (base + kn * wn) * wet_c * wn
-            coef[at + 3] = 0.5 * (ks * ws + base) * ws * wet_c
+        return wet_c, we, ww, wn, ws
+
+    def faces(row, slot, at):
+        wet_c, we, ww, wn, ws = wet_sides()
+        center = grid[slot]
+        rim_row(row, 5)
+        ke, kw, kn, ks = shifted(center, *side_rows(0, row), grid[5])
+        base = center * wet_c
+        coef[at] = 0.5 * (base + ke * we) * wet_c * we
+        coef[at + 1] = 0.5 * (kw * ww + base) * ww * wet_c
+        coef[at + 2] = 0.5 * (base + kn * wn) * wet_c * wn
+        coef[at + 3] = 0.5 * (ks * ws + base) * ws * wet_c
+
+    @pl.when(is_ocean)
+    def _():
+        faces(SURF + 1, 2, 0)
+        wet_c = grid[4]
         coef[4] = (
             1.0 - (coef[0] + coef[1] + coef[2] + coef[3]) - (2.0 * vertical_mix) * wet_c
         )
         coef[5] = vertical_mix * wet_c
+
+    def line_factors():
+        faces(SURF + 2, 3, 6)
+        wet_c = grid[4]
         diagonal = damping + coef[6] + coef[7] + coef[8] + coef[9]
         coef[10] = diagonal
         main = wet_c * diagonal + (1.0 - wet_c)
@@ -501,6 +519,9 @@
     row48 = lax.broadcasted_iota(jnp.int32, (LEV, CY), 0)
     lane48 = lanes_of((LEV, CY))
 
+    def out_ref(s, x):
+        return fin.at[x] if s == NSTEP else fp.at[s, x + 1]
+
     def ocean_step(s, slabs):
         for x in slabs:
             c = fp[s - 1, x + 1, 0:LEV, :]
@@ -523,9 +544,9 @@
                 + row(3) * o
                 + row(5) * (up + down)
             )
-            fp[s, x + 1, 0:LEV, :] = new
+            out_ref(s, x)[0:LEV, :] = new
             if s > 1:
-                fp[s, x + 1, 0:1, :] = new[0:1, :] + grid[7, x : x + 1, :]
+                out_ref(s, x)[0:1, :] = new[0:1, :] + grid[7, x : x + 1, :]
 
     def air_step(s, tiles):
         rows = ROWS if s <= ITERS else LEV
@@ -570,12 +591,12 @@
                     + mix_down * (down - b)
                 )
                 x = x0 + j
-                fp[s, x + 1, 0:rows, :] = new
+                out_ref(s, x)[0:rows, :] = new
                 if s == 1:
                     grid[8, x : x + 1, :] = b[0:1, :]
                     grid[9, x : x + 1, :] = b[SURF : SURF + 1, :]
                 else:
-                    fp[s, x + 1, 0:1, :] = (
+                    out_ref(s, x)[0:1, :] = (
                         new[0:1, :]
                         + grid[6, x : x + 1, :]
                         - grid[7, x : x + 1, :] * b[0:1, :]
@@ -588,9 +609,18 @@
                         )
 
 
+    def apply_a(s, center):
+        wet_c = grid[4]
+        rim_row(SURF, 5)
+        east, west, north, south = shifted(center, *side_rows(s, SURF), grid[5])
+        near = coef[6] * east + coef[7] * west + coef[8] * north + coef[9] * south
+        return wet_c * (coef[10] * center - near) + (1.0 - wet_c) * center
+
     @pl.when(is_ocean)
     def _():
         ocean_step(1, ALL)
+        line_factors()
+        grid[8] = apply_a(0, grid[1])
 
     @pl.when(is_air)
     def _():
@@ -611,14 +641,12 @@
     high, low = split(trecv[...].reshape(sources * 64, 128))
     table[:, 0:128] = high
     table[:, 128:256] = low
-    key_lane = lax.broadcasted_iota(jnp.int32, (units, sources * 64), 1).astype(F32)
     lane256 = lax.broadcasted_iota(jnp.int32, (units, 256), 1)
     low_lane = ((lane256 // 4) % 4).astype(F32)
     slot_of = (lane256 // 16) % 8
     picked = jnp.zeros((units, 256), F32)
     for m in range(SLOTS):
-        hot = jnp.where(key[:, m : m + 1] == key_lane, 1.0, 0.0).astype(BF16)
-        found = dot(hot, table[...])
+        found = dot(hot[m], table[...])
         found = jnp.where(low_lane == tile_low[:, m : m + 1], found, 0.0).astype(BF16)
         picked = jnp.where(slot_of == m, dot(found, cbuf[0:256, :]), picked)
     high, low = split(picked)
@@ -691,12 +719,6 @@
     half_range = (bound_high - bound_low) / 2.0
     spread_ratio = centre / half_range
 
-    def apply_a(s, center):
-        rim_row(SURF, 5)
-        east, west, north, south = shifted(center, *side_rows(s, SURF), grid[5])
-        near = coef[6] * east + coef[7] * west + coef[8] * north + coef[9] * south
-        return wet_c * (coef[10] * center - near) + (1.0 - wet_c) * center
-
     def put_surface(s, value):
         grid[13] = value
         if s < ITERS:
@@ -715,7 +737,7 @@
         pack_inner(1, INNER, LEVELS)
         send(1, INSIDE)
         eta = grid[1]
-        residual = wet_c * (damping * eta + fresh_rate * imp[1]) - apply_a(0, eta)
+        residual = wet_c * (damping * eta + fresh_rate * imp[1]) - grid[8]
         direction = solve(residual) / centre
         grid[11] = eta + direction
         grid[12] = residual
@@ -809,9 +831,6 @@
                 gather_row(s, SURF, 11)
 
         recurrence = recurrence_next
-        if s == ITERS:
-            loads["surface"] = [pltpu.make_async_copy(grid.at[11], surface_out.at[0], lsem.at[41])]
-            loads["surface"][0].start()
         phase = s - 2
         if phase < phases:
             sum_finish(phase)
@@ -831,21 +850,10 @@
             spread = jnp.where(row8 == k, response[k], spread)
         spread = spread * correction
 
-        def body(x, carry):
-            fp[NSTEP, x + 1, 0:8, :] = (
-                fp[NSTEP, x + 1, 0:8, :] + spread * grid[4, pl.ds(x, 1), :]
-            )
-            return carry
-
-        lax.fori_loop(0, CX, body, 0)
-
-    stores = []
-    for x in range(CX):
-        copy = pltpu.make_async_copy(
-            fp.at[NSTEP, x + 1, pl.ds(0, LEV), :], theta_out.at[0, :, x, :], lsem.at[8 + x]
-        )
-        copy.start()
-        stores.append(copy)
+        for x in range(CX):
+            fin[x, 0:8, :] = fin[x, 0:8, :] + spread * grid[4, x : x + 1, :]
+
+    surface_fin[...] = grid[11]
     for s in range(NSTEP):
         drain_halo(s)
     for d, j, peer in export_peers:
@@ -853,8 +861,15 @@
     for phase in range(phases):
         for j in range(len(sum_phases[phase])):
             sum_copy(phase, j).wait_send()
-    loaded("surface")
-    for copy in stores:
+
+
+def store_kernel(fin, surface_fin, theta_out, surface_out, sem):
+    copies = [pltpu.make_async_copy(surface_fin, surface_out.at[0], sem.at[CX])]
+    for x in range(CX):
+        copies.append(pltpu.make_async_copy(fin.at[x], theta_out.at[0, :, x, :], sem.at[x]))
+    for copy in copies:
+        copy.start()
+    for copy in copies:
         copy.wait()
 
 
@@ -869,16 +884,21 @@
     def per_device(theta, surface, kappa, depth, wet, ids, counts, weights):
         spec = pl.BlockSpec(memory_space=pl.ANY)
         dma = pltpu.SemaphoreType.DMA
-        return pl.pallas_call(
+        near = pl.BlockSpec(memory_space=pltpu.VMEM)
+        hbm = lambda v: pltpu.with_memory_space_constraint(v, pltpu.HBM)
+        theta, surface, kappa, depth, wet, ids, counts, weights = map(
+            hbm, (theta, surface, kappa, depth, wet, ids.transpose(0, 1, 3, 2), counts, weights)
+        )
+        fields = pl.pallas_call(
             functools.partial(kernel, n_gx, n_gy),
             out_shape=(
-                jax.ShapeDtypeStruct((1, LEV, CX, CY), F32),
-                jax.ShapeDtypeStruct((1, CX, CY), F32),
+                jax.ShapeDtypeStruct((CX, LEV, CY), F32),
+                jax.ShapeDtypeStruct((CX, CY), F32),
             ),
             in_specs=[spec] * 9,
-            out_specs=(spec, spec),
+            out_specs=(near, near),
             scratch_shapes=[
-                pltpu.VMEM((NSTEP + 1, CX + 2, ROWS, CY), F32),
+                pltpu.VMEM((NSTEP, CX + 2, ROWS, CY), F32),
                 pltpu.VMEM((NSTEP, 4, 8, CY), F32),
                 pltpu.VMEM((NSTEP, 2, 4, 8, CY), F32),
                 pltpu.VMEM((NSTEP, 8, CY), F32),
@@ -895,6 +915,7 @@
                 pltpu.VMEM((CX, CY), jnp.int32),
                 pltpu.VMEM((11, CX, CY), F32),
                 pltpu.VMEM((4, 256, 128), BF16),
+                pltpu.VMEM((SLOTS, 256, sources * 64), BF16),
                 pltpu.VMEM((2, 4, 8, 128), F32),
                 pltpu.VMEM((2, CX, CY), F32),
                 pltpu.VMEM((15, CX, CY), F32),
@@ -910,7 +931,7 @@
                 dma((phases, widest)),
             ],
             compiler_params=pltpu.CompilerParams(
-                collective_id=0, has_side_effects=True, vmem_limit_bytes=60 * 1024 * 1024
+                collective_id=0, has_side_effects=True, vmem_limit_bytes=36 * 1024 * 1024
             ),
         )(
             theta,
@@ -918,11 +939,22 @@
             kappa,
             depth,
             wet,
-            ids.transpose(0, 1, 3, 2),
+            ids,
             counts,
             weights,
-            jnp.asarray(constants),
+            hbm(jnp.asarray(constants)),
         )
+        return pl.pallas_call(
+            store_kernel,
+            out_shape=(
+                jax.ShapeDtypeStruct((1, LEV, CX, CY), F32),
+                jax.ShapeDtypeStruct((1, CX, CY), F32),
+            ),
+            in_specs=[near, near],
+            out_specs=(spec, spec),
+            scratch_shapes=[dma((CX + 1,))],
+            compiler_params=pltpu.CompilerParams(vmem_limit_bytes=8 * 1024 * 1024),
+        )(*fields)
 
     in_specs = (
         P("comp", None, "gx", "gy"),

time: 57.4 us -> 54.2 us (0.944)
  local copies, waits for them, and re-layouts: 2.68 us -> 0 us
  Pallas kernels: 53.9 us -> 53.3 us
    unnamed x4 -> x0, local copies, waits for them, and re-layouts: 2.68 us -> none
    pallas_call x1, Pallas kernels: 53.9 us -> 52.1 us  [per_device(): pl.pallas_call(functools.partial(kernel, n_gx, n_gy), out_shape=(jax.Shap...]
    pallas_call x0 -> x1, Pallas kernels: none -> 1.15 us  [per_device(): pl.pallas_call(store_kernel, out_shape=(jax.ShapeDtypeStruct((1, LEV, CX,...]
where the time goes in v3:
time: 54.2 us; the launch traced here: 54.1 us
  Pallas kernels  53.3 us (98%)
  between operations  0.8 us (1%)
    pallas_call x1, Pallas kernels, per_device(): pl.pallas_call(functools.partial(kernel, n_gx, n_gy), out_shape=(jax.Shap...  52.1 us
    pallas_call x1, Pallas kernels, per_device(): pl.pallas_call(store_kernel, out_shape=(jax.ShapeDtypeStruct((1, LEV, CX,...  1.15 us

profile of v3, /device:TPU:1, one launch (start us, length us, event | category | flops | bytes accessed | tf_op | source)
XLA Modules:
  0.0 54.1 jit_solution(1326955341506562796)
XLA Ops:
  0.6 52.1 %shard_map.104 = (f32[32,48,128]{2,1,0:T(8,128)S(1)}, f32[32,128]{1,0:T(8,128)S(1)}) custom-call(f32[1,48,32,128]{3,2,1,0:T(8,128)} %theta.1, f32[1,32,128]{2,1,0:T(8,128)} %surface.1, f32[1,32,128]{2,1,0:T(8,128)} %kappa.1, f32[32,128]{1,0:T(8,128)} %depth.1, s32[32,128]{1,0:T(8,128)} %wet.1, s32[1,8,8,32]{3,2,1,0:T(8,128)} %bitcast.1, s32[1,8,32]{2,1,0:T(8,128)} %counts.1, ...), custom_call_target="tpu_custom_call" | custom-call | tf_op jit(solution)/shard_map/pallas_call | solution.py:892
  52.8 1.2 %shard_map.105 = (f32[1,48,32,128]{3,2,1,0:T(8,128)}, f32[1,32,128]{2,1,0:T(8,128)}) custom-call(f32[32,48,128]{2,1,0:T(8,128)S(1)} %get-tuple-element.4.fin, f32[32,128]{1,0:T(8,128)S(1)} %get-tuple-element.5.surface_fin), custom_call_target="tpu_custom_call" | custom-call | tf_op jit(solution)/shard_map/pallas_call | solution.py:947

commit v4 on v3

--- a/solution.py
+++ b/solution.py
@@ -120,6 +120,7 @@
     yr,
     ye,
     yer,
+    yc,
     zb,
     ex,
     tsend,
@@ -262,6 +263,16 @@
                 acc = place_in(acc, moved, lane)
         ye[s] = acc
 
+    def pack_corner(s, side, blocks):
+        e = 7 * side
+        acc = jnp.zeros((8, 128), F32)
+        for b in blocks:
+            lane = 16 * b + 2 * e
+            x = EDGE[e]
+            moved = pltpu.roll(fp[s, x + 1, 8 * b : 8 * b + 8, :], lane + 1, 1)
+            acc = place_in(acc, moved, lane)
+        yc[s, side] = acc
+
     def merge(low, high):
         return jnp.where(lane128 % 2 == 0, low, pltpu.roll(high, 126, 1))
 
@@ -283,12 +294,13 @@
             for e, x in enumerate(EDGE):
                 zb[x + 1, 8 * b : 8 * b + 8, :] = turn(both, 16 * b + 2 * e)
 
-    def unpack_corner(s, blocks):
-        west = merge(yer[s, 2], yer[s, 4])
-        east = merge(yer[s, 3], yer[s, 5])
+    def unpack_corner(s, side, blocks):
+        both = merge(yer[s, 2 + side], yer[s, 4 + side])
         for b in blocks:
-            zb[0, 8 * b : 8 * b + 8, :] = turn(west, 16 * b + 14)
-            zb[CX + 1, 8 * b : 8 * b + 8, :] = turn(east, 16 * b)
+            if side:
+                zb[CX + 1, 8 * b : 8 * b + 8, :] = turn(both, 16 * b)
+            else:
+                zb[0, 8 * b : 8 * b + 8, :] = turn(both, 16 * b + 14)
 
     def copy_to(s, d):
         peer = halo_peers[d % 2 if d < 4 else 2 + d % 2 if d < 10 else d - 6]
@@ -303,7 +315,7 @@
         elif d < 10:
             src, dst = ys.at[s, 3], yr.at[s, d - 8, 3]
         else:
-            src, dst = ye.at[s], yer.at[s, d - 8]
+            src, dst = yc.at[s, 1 - d % 2], yer.at[s, d - 8]
         return pltpu.make_async_remote_copy(
             src_ref=src,
             dst_ref=dst,
@@ -355,16 +367,17 @@
     BOTH = tuple(range(7))
     loaded("theta")
     pack_edge(0, BOTH)
+    pack_corner(0, 0, BOTH)
+    pack_corner(0, 1, BOTH)
     pack_inner(0, INNER, LEVELS)
     pack_inner(0, ALL, (6,))
     pl.semaphore_wait(barrier, len(greeted))
-    send(0, SLAB, SLAB_SURF, OUTER)
 
     @pl.when(is_air)
     def _():
         send(0, CORNER)
 
-    send(0, INSIDE, SURF_COLUMN)
+    send(0, SLAB, SLAB_SURF, OUTER, INSIDE, SURF_COLUMN)
     for d, j, peer in export_peers:
         if d:
             export_copy(d, j, peer).start()
@@ -419,7 +432,8 @@
     @pl.when(is_air)
     def _():
         wait(0, CORNER)
-        unpack_corner(0, BOTH)
+        unpack_corner(0, 0, BOTH)
+        unpack_corner(0, 1, BOTH)
 
 
     def lanes_of(shape):
@@ -758,9 +772,11 @@
             fp[1, x + 1, SURF : SURF + 1, :] = (
                 fp[1, x + 1, SURF : SURF + 1, :] + grid[11, x : x + 1, :]
             )
-        send(1, SLAB, SLAB_SURF)
+        pack_corner(1, 0, BOTH)
+        pack_corner(1, 1, BOTH)
+        send(1, CORNER, SLAB, SLAB_SURF)
         pack_edge(1, BOTH)
-        send(1, CORNER, OUTER)
+        send(1, OUTER)
         pack_inner(1, INNER, BOTH)
         send(1, INSIDE, SURF_COLUMN)
 
@@ -793,11 +809,15 @@
                     send(s, SLAB_SURF)
                     pack_inner(s, ALL, (6,))
                     send(s, SURF_COLUMN)
-            wait(s - 1, OUTER, SLAB)
+            wait(s - 1, OUTER)
             unpack_edge(s - 1, LEVELS)
-            ocean_step(s, EDGE)
+            ocean_step(s, EDGE[1:-1])
+            for side, x in ((0, 0), (1, CX - 1)):
+                wait(s - 1, (side,))
+                ocean_step(s, (x,))
+                if not last:
+                    send(s, (1 - side,))
             if not last:
-                send(s, SLAB)
                 pack_edge(s, LEVELS)
                 send(s, OUTER)
 
@@ -816,17 +836,20 @@
                 send(s, INSIDE)
                 if s < ITERS:
                     send(s, SURF_COLUMN)
-            wait(s - 1, SLAB, CORNER)
-            if s <= ITERS:
-                wait(s - 1, SLAB_SURF)
-            unpack_corner(s - 1, used)
+            for side in (0, 1):
+                wait(s - 1, (side,), (10 + side, 12 + side))
+                if s <= ITERS:
+                    wait(s - 1, (2 + side,))
+                unpack_corner(s - 1, side, used)
             air_step(s, (0, CX // 4 - 1))
             if not last:
-                send(s, SLAB)
+                pack_corner(s, 0, made)
+                pack_corner(s, 1, made)
+                send(s, CORNER, SLAB)
                 if s < ITERS:
                     send(s, SLAB_SURF)
                 pack_edge(s, made)
-                send(s, CORNER, OUTER)
+                send(s, OUTER)
             if s == ITERS:
                 gather_row(s, SURF, 11)
 
@@ -903,6 +926,7 @@
                 pltpu.VMEM((NSTEP, 2, 4, 8, CY), F32),
                 pltpu.VMEM((NSTEP, 8, CY), F32),
                 pltpu.VMEM((NSTEP, 6, 8, CY), F32),
+                pltpu.VMEM((NSTEP, 2, 8, CY), F32),
                 pltpu.VMEM((CX + 2, ROWS, CY), F32),
                 pltpu.VMEM((2, CX, CY), F32),
                 pltpu.VMEM((64, 128), F32),

time: 54.2 us -> 53.4 us (0.985)
  Pallas kernels: 53.3 us -> 52.5 us
    pallas_call x1, Pallas kernels: 52.1 us -> 51.3 us  [per_device(): pl.pallas_call(functools.partial(kernel, n_gx, n_gy), out_shape=(jax.Shap...]
where the time goes in v4:
time: 53.4 us; the launch traced here: 53.3 us
  Pallas kernels  52.5 us (98%)
  between operations  0.8 us (1%)
    pallas_call x1, Pallas kernels, per_device(): pl.pallas_call(functools.partial(kernel, n_gx, n_gy), out_shape=(jax.Shap...  51.3 us
    pallas_call x1, Pallas kernels, per_device(): pl.pallas_call(store_kernel, out_shape=(jax.ShapeDtypeStruct((1, LEV, CX,...  1.15 us

profile of v4, /device:TPU:1, one launch (start us, length us, event | category | flops | bytes accessed | tf_op | source)
XLA Modules:
  0.0 53.3 jit_solution(18048938527972375055)
XLA Ops:
  0.6 51.3 %shard_map.104 = (f32[32,48,128]{2,1,0:T(8,128)S(1)}, f32[32,128]{1,0:T(8,128)S(1)}) custom-call(f32[1,48,32,128]{3,2,1,0:T(8,128)} %theta.1, f32[1,32,128]{2,1,0:T(8,128)} %surface.1, f32[1,32,128]{2,1,0:T(8,128)} %kappa.1, f32[32,128]{1,0:T(8,128)} %depth.1, s32[32,128]{1,0:T(8,128)} %wet.1, s32[1,8,8,32]{3,2,1,0:T(8,128)} %bitcast.1, s32[1,8,32]{2,1,0:T(8,128)} %counts.1, ...), custom_call_target="tpu_custom_call" | custom-call | tf_op jit(solution)/shard_map/pallas_call | solution.py:915
  51.9 1.2 %shard_map.105 = (f32[1,48,32,128]{3,2,1,0:T(8,128)}, f32[1,32,128]{2,1,0:T(8,128)}) custom-call(f32[32,48,128]{2,1,0:T(8,128)S(1)} %get-tuple-element.4.fin, f32[32,128]{1,0:T(8,128)S(1)} %get-tuple-element.5.surface_fin), custom_call_target="tpu_custom_call" | custom-call | tf_op jit(solution)/shard_map/pallas_call | solution.py:971
